TPU v7x, 128 devices: a whole 4x4x4 slice. The times are simulated.
128 devices in a mesh: rows: 32 (over x, z, core), cols: 4 (over y).
Axes of the slice: x: 4, y: 4, z: 4, core: 2. Of those that a mesh axis runs over, the one named last changes fastest.
Arguments:
- points: float32 [98304, 1024], P('rows', 'cols'), may hold values from -80 to 80
- codes: int32 [128, 98304], P('cols', 'rows'), may hold values from 0 to 255, as said below
- rotation: float32 [1024, 1024], P('rows', 'cols'), may hold values from -0.16 to 1.16
Outputs:
- new_rotation: float32 [1024, 1024], P('rows', 'cols')
- centroids: float32 [128, 2048], P('cols')
Inputs may be any that keep to these rules, and one draw needn't show every extreme that they name: For every subspace, the first 256 vectors hold each of the 256 codes once.
All inputs are finite; a program needn't handle non-finite values.
Results may differ from a plain program's by a relative error of at most 0.00011.
Values sent between devices are 32-bit elements; how exact they have to be, the bound alone decides.
No kernel may reach another device: no remote copies, remote signals or barrier semaphores. Data moves between devices by JAX's collectives and lax.ppermute only.
A program may use at most 128 MiB of HBM per device.

v0:
```python
import jax
import jax.numpy as jnp
from jax import lax
from jax.sharding import PartitionSpec as P

D = 1024
K = 256
NS_ITERS = 6
SUB = 8


def contract_rows(left, right):
    return lax.dot_general(
        left,
        right,
        (((0,), (0,)), ((), ())),
        precision=lax.Precision.HIGHEST,
        preferred_element_type=jnp.float32,
    )


def matmul_high(left, right):
    return jnp.dot(left, right, precision=lax.Precision.HIGHEST, preferred_element_type=jnp.float32)


def gram_parts(current):
    row_block = lax.all_gather(current, "cols", axis=1, tiled=True)
    partial_gram = contract_rows(row_block, current)
    return (row_block, lax.psum(partial_gram, "rows"))


def shards(points, codes, rotation):
    gathered = lax.all_gather(points, "cols", axis=1, tiled=True)
    column_panel = lax.all_gather(rotation, "rows", axis=0, tiled=True)
    rotated = matmul_high(gathered, column_panel)
    local_subspaces = codes.shape[0]
    vector_count = rotated.shape[0]
    panel_width = rotated.shape[1]
    batch_size = 4
    turn_count = local_subspaces // batch_size
    code_range = jnp.arange(K, dtype=jnp.int32)
    rotated_groups = rotated.reshape(vector_count, turn_count, batch_size, SUB).transpose(
        1, 2, 0, 3
    )
    code_groups = codes.reshape(turn_count, batch_size, vector_count)

    def local_totals(carry, item):
        block_values, code_block = item
        indicator = (code_block[:, :, None] == code_range[None, None, :]).astype(jnp.float32)
        value_sums = jnp.einsum(
            "gnk,gns->gks",
            indicator,
            block_values,
            precision=lax.Precision.HIGHEST,
            preferred_element_type=jnp.float32,
        )
        return (carry, (value_sums, jnp.sum(indicator, axis=1)))

    unused, (value_totals, code_totals) = lax.scan(local_totals, 0.0, (rotated_groups, code_groups))
    value_totals = value_totals.reshape(local_subspaces, K * SUB)
    code_totals = code_totals.reshape(local_subspaces, K)
    owned_values, owned_counts = (
        lax.psum_scatter(value_totals, "rows", scatter_dimension=0, tiled=True),
        lax.psum_scatter(code_totals, "rows", scatter_dimension=0, tiled=True),
    )
    owned_centers = (owned_values.reshape(-1, K, SUB) / owned_counts[:, :, None]).reshape(
        -1, K * SUB
    )
    centroids = lax.all_gather(owned_centers, "rows", axis=0, tiled=True)
    center_groups = centroids.reshape(turn_count, batch_size, K, SUB)

    def rebuild(carry, item):
        code_block, center_block = item
        indicator = (code_block[:, :, None] == code_range[None, None, :]).astype(jnp.float32)
        return (
            carry,
            jnp.einsum(
                "gnk,gks->gns",
                indicator,
                center_block,
                precision=lax.Precision.HIGHEST,
                preferred_element_type=jnp.float32,
            ),
        )

    unused, rebuilt = lax.scan(rebuild, 0.0, (code_groups, center_groups))
    approx = rebuilt.transpose(2, 0, 1, 3).reshape(vector_count, panel_width)
    cross_block = lax.psum_scatter(
        contract_rows(gathered, approx), "rows", scatter_dimension=0, tiled=True
    )
    square_total = lax.psum(jnp.sum(cross_block * cross_block), ("rows", "cols"))
    iterate = 1.7 * cross_block / jnp.sqrt(square_total + 1e-06)
    for step_index in range(NS_ITERS):
        row_block, gram_panel = gram_parts(iterate)
        iterate = 1.5 * iterate - 0.5 * matmul_high(row_block, gram_panel)
    return (iterate * D**0.5, centroids)


def solution(mesh):
    in_specs = (P("rows", "cols"), P("cols", "rows"), P("rows", "cols"))
    out_specs = (P("rows", "cols"), P("cols", None))
    return jax.shard_map(shards, mesh=mesh, in_specs=in_specs, out_specs=out_specs, check_vma=False)
```

profile of v0, /device:TPU:6, one launch (start us, length us, event | category | flops | bytes accessed | tf_op | source)
XLA Modules:
  0.0 1367.0 jit_solution(11022926561968581953)
XLA Ops:
  8.9 46.3 %all-gather.6.cloned.1.call-done = f32[1024,256]{1,0:T(8,128)} async-done(((f32[32,256]{1,0:T(8,128)}), f32[1024,256]{1,0:T(8,128)}) %all-gather.6.cloned.1.call-update) | async-done | bytes 1048592 | tf_op jit(solution)/shard_map/all_gather | solution.py:34
  55.2 119.8 %all-gather.4.cloned.1.call-done = f32[3072,1024]{1,0:T(8,128)} async-done(((f32[3072,256]{1,0:T(8,128)}), f32[3072,1024]{1,0:T(8,128)}) %all-gather.4.cloned.1.call-update) | async-done | bytes 12582928 | tf_op jit(solution)/shard_map/all_gather | solution.py:33
  175.0 13.8 %fusion.28 = f32[3072,256]{0,1:T(8,128)S(1)} fusion(f32[3072,1024]{1,0:T(8,128)} %all-gather.4.cloned.1.call-done, f32[1024,256]{1,0:T(8,128)} %all-gather.6.cloned.1.call-done), kind=kOutput, calls=%fused_computation.43 | convolution fusion | flops 9663676416 | bytes 16777216 | tf_op jit(solution)/shard_map/dot_general | solution.py:23
  188.8 63.4 %while.24 = (s32[]{:T(128)}, f32[8,4,256,8]{2,3,1,0:T(8,128)}, f32[8,4,256]{2,1,0:T(4,128)}, s32[8,4,3072]{2,1,0:T(4,128)S(1)}, f32[8,4,3072,8]{2,3,1,0:T(8,128)S(1)}, /*index=5*/s32[]{:T(128)}) while((s32[]{:T(128)}, f32[8,4,256,8]{2,3,1,0:T(8,128)}, f32[8,4,256]{2,1,0:T(4,128)}, s32[8,4,3072]{2,1,0:T(4,128)S(1)}, ...), condition=%wide.region_2.3_spmd.clone, body=%wide.region_0.2_spmd.clone.sunk | while | flops 314571776 | bytes 636489 | solution.py:59
  188.9 5.1 fusion.69
  193.9 2.3 fusion.70
  196.8 5.0 fusion.69
  201.8 2.3 fusion.70
  204.7 5.0 fusion.69
  209.8 2.3 fusion.70
  212.6 5.0 fusion.69
  217.7 2.3 fusion.70
  220.6 5.0 fusion.69
  225.6 2.3 fusion.70
  228.5 5.0 fusion.69
  236.4 5.0 fusion.69
  244.3 5.0 fusion.69
  252.2 3.5 copy.22
  255.7 4.7 reshape.46
  261.9 109.6 %all-reduce.1 = f32[32,256]{1,0:T(8,128)S(1)} all-reduce(f32[32,256]{1,0:T(8,128)S(1)} %reshape.47), channel_id=3, replica_groups=mesh['rows'=32,'cols'=4] {'rows'}, use_global_device_ids=true, to_apply=%region_4.5.clone | all-reduce | flops 8192 | bytes 65536
  374.1 41.1 %all-gather = f32[32,1,2048]{2,1,0:T(1,128)S(1)} all-gather(f32[1,1,2048]{2,1,0:T(1,128)S(1)} %fusion.27), channel_id=1, replica_groups=mesh['rows'=32,'cols'=4] {'rows'}, dimensions={0}, use_global_device_ids=true | all-gather | bytes 270336 | tf_op jit(solution)/shard_map/all_gather | solution.py:69
  415.7 3.7 reshape.48
  419.4 2.8 copy.23
  422.2 59.3 %while.25 = (s32[]{:T(128)}, f32[8,4,3072,8]{2,3,1,0:T(8,128)}, s32[8,4,3072]{2,1,0:T(4,128)S(1)}, f32[8,4,256,8]{2,3,1,0:T(8,128)S(1)}, s32[]{:T(128)}) while((s32[]{:T(128)}, f32[8,4,3072,8]{2,3,1,0:T(8,128)}, s32[8,4,3072]{2,1,0:T(4,128)S(1)}, f32[8,4,256,8]{2,3,1,0:T(8,128)S(1)}, s32[]{:T(128)}) %tuple.73), condition=%wide.region_6.7_spmd.clone, body=%wide.region_5.6_spmd.clone.sunk | while | flops 305135616 | bytes 574529 | solution.py:86
  422.2 7.4 fusion.72
  429.6 7.4 fusion.72
  437.0 7.4 fusion.72
  444.4 7.4 fusion.72
  451.8 7.4 fusion.72
  459.2 7.4 fusion.72
  466.6 7.4 fusion.72
  474.0 7.4 fusion.72
  481.4 13.6 convolution_bitcast_fusion
  496.5 76.6 %reduce-scatter.4.cloned.1.call-done = f32[32,256]{1,0:T(8,128)} async-done(((f32[1024,256]{1,0:T(8,128)}), f32[32,256]{1,0:T(8,128)}) %reduce-scatter.4.cloned.1.call-update) | async-done | bytes 32784 | tf_op jit(solution)/shard_map/reduce_scatter | solution.py:88
  574.6 62.3 %psum.49 = f32[]{:T(128)} all-reduce(f32[]{:T(128)} %multiply_reduce_fusion), channel_id=1, replica_groups=mesh['rows'=32,'cols'=4] {'rows','cols'}, use_global_device_ids=true, to_apply=%region_9.10 | all-reduce | flops 1 | bytes 8 | tf_op jit(solution)/shard_map/psum | solution.py:91
  638.3 12.0 all_gather.30
  652.4 105.1 %all-reduce.10.cloned.1.call-done = f32[1024,256]{1,0:T(8,128)} async-done(((f32[1024,256]{1,0:T(8,128)}), f32[1024,256]{1,0:T(8,128)}) %all-reduce.10.cloned.1.call-update) | async-done | bytes 1048592 | tf_op jit(solution)/shard_map/psum | solution.py:29
  759.4 12.4 all_gather.31
  773.9 103.6 %all-reduce.12.cloned.1.call-done = f32[1024,256]{1,0:T(8,128)} async-done(((f32[1024,256]{1,0:T(8,128)}), f32[1024,256]{1,0:T(8,128)}) %all-reduce.12.cloned.1.call-update) | async-done | bytes 1048592 | tf_op jit(solution)/shard_map/psum | solution.py:29
  879.4 12.6 all_gather.32
  894.1 103.7 %all-reduce.14.cloned.1.call-done = f32[1024,256]{1,0:T(8,128)} async-done(((f32[1024,256]{1,0:T(8,128)}), f32[1024,256]{1,0:T(8,128)}) %all-reduce.14.cloned.1.call-update) | async-done | bytes 1048592 | tf_op jit(solution)/shard_map/psum | solution.py:29
  999.6 12.4 all_gather.33
  1014.1 103.7 %all-reduce.16.cloned.1.call-done = f32[1024,256]{1,0:T(8,128)} async-done(((f32[1024,256]{1,0:T(8,128)}), f32[1024,256]{1,0:T(8,128)}) %all-reduce.16.cloned.1.call-update) | async-done | bytes 1048592 | tf_op jit(solution)/shard_map/psum | solution.py:29
  1119.6 12.4 all_gather.34
  1134.1 103.7 %all-reduce.18.cloned.1.call-done = f32[1024,256]{1,0:T(8,128)} async-done(((f32[1024,256]{1,0:T(8,128)}), f32[1024,256]{1,0:T(8,128)}) %all-reduce.18.cloned.1.call-update) | async-done | bytes 1048592 | tf_op jit(solution)/shard_map/psum | solution.py:29
  1239.6 12.4 all_gather.35
  1254.8 102.9 %all-reduce.20.cloned.1.call-done = f32[1024,256]{1,0:T(8,128)} async-done(((f32[1024,256]{1,0:T(8,128)}), f32[1024,256]{1,0:T(8,128)}) %all-reduce.20.cloned.1.call-update) | async-done | bytes 1048592 | tf_op jit(solution)/shard_map/psum | solution.py:29
  1357.7 2.4 fusion.21
  (79 shorter events, 44.0 us)
Async XLA Ops:
  7.2 1.6 copy-start
  7.2 48.0 %all-gather.6.cloned.1.call-start = ((), (), s32[]{:S(2)}) async-start(), calls=%async_computation.2 | async-start | bytes 1081344 | tf_op jit(solution)/shard_map/all_gather | solution.py:34
  7.9 167.1 %all-gather.4.cloned.1.call-start = ((), (), s32[]{:S(2)}) async-start(), calls=%async_computation.1 | async-start | bytes 15728640 | tf_op jit(solution)/shard_map/all_gather | solution.py:33
  8.7 363.8 %all-reduce.22.cloned.1.call-start = ((), (), s32[]{:S(2)}) async-start(), calls=%async_computation.10 | async-start | bytes 524288
  255.7 4.8 copy-start.1
  260.4 312.7 %reduce-scatter.4.cloned.1.call-start = ((), (), s32[]{:S(2)}) async-start(), calls=%async_computation.9 | async-start | bytes 1081344 | tf_op jit(solution)/shard_map/reduce_scatter | solution.py:88
  496.4 261.1 %all-reduce.10.cloned.1.call-start = ((), (), s32[]{:S(2)}) async-start(), calls=%async_computation.3 | async-start | bytes 2097152 | tf_op jit(solution)/shard_map/psum | solution.py:29
  652.4 225.2 %all-reduce.12.cloned.1.call-start = ((), (), s32[]{:S(2)}) async-start(), calls=%async_computation.4 | async-start | bytes 2097152 | tf_op jit(solution)/shard_map/psum | solution.py:29
  773.8 223.9 %all-reduce.14.cloned.1.call-start = ((), (), s32[]{:S(2)}) async-start(), calls=%async_computation.5 | async-start | bytes 2097152 | tf_op jit(solution)/shard_map/psum | solution.py:29
  894.1 223.7 %all-reduce.16.cloned.1.call-start = ((), (), s32[]{:S(2)}) async-start(), calls=%async_computation.6 | async-start | bytes 2097152 | tf_op jit(solution)/shard_map/psum | solution.py:29
  1014.1 223.7 %all-reduce.18.cloned.1.call-start = ((), (), s32[]{:S(2)}) async-start(), calls=%async_computation.7 | async-start | bytes 2097152 | tf_op jit(solution)/shard_map/psum | solution.py:29
  1134.0 223.7 %all-reduce.20.cloned.1.call-start = ((), (), s32[]{:S(2)}) async-start(), calls=%async_computation.8 | async-start | bytes 2097152 | tf_op jit(solution)/shard_map/psum | solution.py:29
Sparse Core Ops, SparseCore 0:
  10.3 44.8 all-gather.5
  56.8 118.0 all-gather.3
  260.5 103.2 all-reduce.21
  496.5 76.4 reduce-scatter.3
  652.5 105.0 all-reduce.9
  774.0 103.5 all-reduce.11
  894.2 103.5 all-reduce.13
  1014.2 103.5 all-reduce.15
  1134.2 103.5 all-reduce.17
  1254.2 103.5 all-reduce.19
where the time goes:
time: 1370 us
  waiting for transfers between devices  867 us (63%)
  blocking collectives  287 us (21%)
  matrix products  151 us (11%)
  local copies, waits for them, and re-layouts  24.9 us (2%)
  other arithmetic  21.8 us (2%)
  between operations  15 us (1%)
    psum x6, waiting for transfers between devices, gram_parts(): return (row_block, lax.psum(partial_gram, 'rows'))  623 us
    all_gather x1, waiting for transfers between devices, shards(): gathered = lax.all_gather(points, 'cols', axis=1, tiled=True)  120 us
    unnamed x1, blocking collectives  110 us
    reduce_scatter x1, waiting for transfers between devices, shards(): lax.psum_scatter(contract_rows(gathered, approx), 'rows', scatter_dimensi...  76.6 us
    all_gather x6, blocking collectives, gram_parts(): row_block = lax.all_gather(current, 'cols', axis=1, tiled=True)  74.1 us
    psum x1, blocking collectives, shards(): lax.psum(jnp.sum(cross_block * cross_block), ('rows', 'cols'))  62.3 us
    dot_general x8, matrix products, rebuild(): jnp.einsum('gnk,gks->gns', indicator, center_block, precision=lax.Precisi...  59.2 us
    all_gather x1, waiting for transfers between devices, shards(): column_panel = lax.all_gather(rotation, 'rows', axis=0, tiled=True)  46.3 us
  transfers between devices with their start and end apart: 10, of which 9 were waited for; matrix products, arithmetic and copies ran while one was open for 0% of the time, Pallas kernels for 0%

commit v1 on v0

--- a/solution.py
+++ b/solution.py
@@ -26,7 +26,7 @@
 def gram_parts(current):
     row_block = lax.all_gather(current, "cols", axis=1, tiled=True)
     partial_gram = contract_rows(row_block, current)
-    return (row_block, lax.psum(partial_gram, "rows"))
+    return (row_block, jnp.sum(lax.all_gather(partial_gram, "rows"), 0))
 
 
 def shards(points, codes, rotation):

time: 1370 us -> 1490 us (1.088)
  other arithmetic: 21.8 us -> 93.4 us
  waiting for transfers between devices: 867 us -> 920 us
    all_gather x0 -> x6, waiting for transfers between devices: none -> 676 us  [gram_parts(): return (row_block, jnp.sum(lax.all_gather(partial_gram, 'rows'), 0))]
    psum x6 -> x0, waiting for transfers between devices: 623 us -> none  [gram_parts(): return (row_block, lax.psum(partial_gram, 'rows'))]
    reduce_sum x0 -> x6, other arithmetic: none -> 71.6 us  [gram_parts(): return (row_block, jnp.sum(lax.all_gather(partial_gram, 'rows'), 0))]
where the time goes in v1:
time: 1490 us; the launch traced here: 1480 us
  waiting for transfers between devices  920 us (62%)
  blocking collectives  287 us (19%)
  matrix products  143 us (10%)
  other arithmetic  93.4 us (6%)
  local copies, waits for them, and re-layouts  25.1 us (2%)
  between operations  15.1 us (1%)
    all_gather x6, waiting for transfers between devices, gram_parts(): return (row_block, jnp.sum(lax.all_gather(partial_gram, 'rows'), 0))  676 us
    all_gather x1, waiting for transfers between devices, shards(): gathered = lax.all_gather(points, 'cols', axis=1, tiled=True)  120 us
    unnamed x1, blocking collectives  110 us
    reduce_scatter x1, waiting for transfers between devices, shards(): lax.psum_scatter(contract_rows(gathered, approx), 'rows', scatter_dimensi...  76.6 us
    all_gather x6, blocking collectives, gram_parts(): row_block = lax.all_gather(current, 'cols', axis=1, tiled=True)  73.7 us
    reduce_sum x6, other arithmetic, gram_parts(): return (row_block, jnp.sum(lax.all_gather(partial_gram, 'rows'), 0))  71.6 us
    psum x1, blocking collectives, shards(): lax.psum(jnp.sum(cross_block * cross_block), ('rows', 'cols'))  62.3 us
    dot_general x8, matrix products, rebuild(): jnp.einsum('gnk,gks->gns', indicator, center_block, precision=lax.Precisi...  59.2 us
  transfers between devices with their start and end apart: 10, of which 9 were waited for; matrix products, arithmetic and copies ran while one was open for 0% of the time, Pallas kernels for 0%

profile of v1, /device:TPU:6, one launch (start us, length us, event | category | flops | bytes accessed | tf_op | source)
XLA Modules:
  0.0 1483.6 jit_solution(13443713318558839122)
XLA Ops:
  9.8 45.4 %all-gather.18.cloned.1.call-done = f32[1024,256]{1,0:T(8,128)} async-done(((f32[32,256]{1,0:T(8,128)}), f32[1024,256]{1,0:T(8,128)}) %all-gather.18.cloned.1.call-update) | async-done | bytes 1048592 | tf_op jit(solution)/shard_map/all_gather | solution.py:34
  55.2 119.8 %all-gather.16.cloned.1.call-done = f32[3072,1024]{1,0:T(8,128)} async-done(((f32[3072,256]{1,0:T(8,128)}), f32[3072,1024]{1,0:T(8,128)}) %all-gather.16.cloned.1.call-update) | async-done | bytes 12582928 | tf_op jit(solution)/shard_map/all_gather | solution.py:33
  175.0 13.8 fusion.28
  188.8 63.4 %while.24 = (s32[]{:T(128)}, f32[8,4,256,8]{2,3,1,0:T(8,128)}, f32[8,4,256]{2,1,0:T(4,128)}, s32[8,4,3072]{2,1,0:T(4,128)S(1)}, f32[8,4,3072,8]{2,3,1,0:T(8,128)S(1)}, /*index=5*/s32[]{:T(128)}) while((s32[]{:T(128)}, f32[8,4,256,8]{2,3,1,0:T(8,128)}, f32[8,4,256]{2,1,0:T(4,128)}, s32[8,4,3072]{2,1,0:T(4,128)S(1)}, ...), condition=%wide.region_2.3_spmd.clone, body=%wide.region_0.2_spmd.clone.sunk | while | flops 314571776 | bytes 635989 | solution.py:59
  191.7 5.0 fusion.69
  199.7 5.0 fusion.69
  207.6 5.0 fusion.69
  215.5 5.0 fusion.69
  223.4 5.0 fusion.69
  231.3 5.0 fusion.69
  239.3 5.0 fusion.69
  247.2 5.0 fusion.69
  252.2 3.5 copy.22
  255.7 4.6 reshape.46
  261.2 110.3 %all-reduce.1 = f32[32,256]{1,0:T(8,128)S(1)} all-reduce(f32[32,256]{1,0:T(8,128)S(1)} %reshape.47), channel_id=9, replica_groups=mesh['rows'=32,'cols'=4] {'rows'}, use_global_device_ids=true, to_apply=%region_4.5.clone | all-reduce | flops 8192 | bytes 65536
  373.9 40.4 %all-gather.6 = f32[32,1,2048]{2,1,0:T(1,128)S(1)} all-gather(f32[1,1,2048]{2,1,0:T(1,128)S(1)} %fusion.27), channel_id=1, replica_groups=mesh['rows'=32,'cols'=4] {'rows'}, dimensions={0}, use_global_device_ids=true | all-gather | bytes 270336 | tf_op jit(solution)/shard_map/all_gather | solution.py:69
  415.0 3.7 reshape.48
  418.6 2.8 copy.23
  421.4 59.3 %while.25 = (s32[]{:T(128)}, f32[8,4,3072,8]{2,3,1,0:T(8,128)}, s32[8,4,3072]{2,1,0:T(4,128)S(1)}, f32[8,4,256,8]{2,3,1,0:T(8,128)S(1)}, s32[]{:T(128)}) while((s32[]{:T(128)}, f32[8,4,3072,8]{2,3,1,0:T(8,128)}, s32[8,4,3072]{2,1,0:T(4,128)S(1)}, f32[8,4,256,8]{2,3,1,0:T(8,128)S(1)}, s32[]{:T(128)}) %tuple.73), condition=%wide.region_6.7_spmd.clone, body=%wide.region_5.6_spmd.clone.sunk | while | flops 305135616 | bytes 574537 | solution.py:86
  421.4 7.4 fusion.72
  428.9 7.4 fusion.72
  436.3 7.4 fusion.72
  443.7 7.4 fusion.72
  451.1 7.4 fusion.72
  458.5 7.4 fusion.72
  465.9 7.4 fusion.72
  473.3 7.4 fusion.72
  480.7 13.6 convolution_bitcast_fusion
  495.7 76.6 %reduce-scatter.4.cloned.1.call-done = f32[32,256]{1,0:T(8,128)} async-done(((f32[1024,256]{1,0:T(8,128)}), f32[32,256]{1,0:T(8,128)}) %reduce-scatter.4.cloned.1.call-update) | async-done | bytes 32784 | tf_op jit(solution)/shard_map/reduce_scatter | solution.py:88
  573.8 62.3 %psum.7 = f32[]{:T(128)} all-reduce(f32[]{:T(128)} %multiply_reduce_fusion), channel_id=1, replica_groups=mesh['rows'=32,'cols'=4] {'rows','cols'}, use_global_device_ids=true, to_apply=%region_9.10 | all-reduce | flops 1 | bytes 8 | tf_op jit(solution)/shard_map/psum | solution.py:91
  637.6 12.0 all_gather.66
  651.6 113.2 %all-gather.20.cloned.1.call-done = f32[32768,256]{1,0:T(8,128)} async-done(((f32[1024,256]{1,0:T(8,128)}), f32[32768,256]{1,0:T(8,128)}) %all-gather.20.cloned.1.call-update) | async-done | bytes 33554448 | tf_op jit(solution)/shard_map/all_gather | solution.py:29
  764.8 11.9 reduce_sum.73
  777.4 12.3 all_gather.69
  792.0 112.6 %all-gather.22.cloned.1.call-done = f32[32768,256]{1,0:T(8,128)} async-done(((f32[1024,256]{1,0:T(8,128)}), f32[32768,256]{1,0:T(8,128)}) %all-gather.22.cloned.1.call-update) | async-done | bytes 33554448 | tf_op jit(solution)/shard_map/all_gather | solution.py:29
  904.6 11.9 reduce_sum.74
  917.1 12.3 all_gather.72
  931.5 112.8 %all-gather.24.cloned.1.call-done = f32[32768,256]{1,0:T(8,128)} async-done(((f32[1024,256]{1,0:T(8,128)}), f32[32768,256]{1,0:T(8,128)}) %all-gather.24.cloned.1.call-update) | async-done | bytes 33554448 | tf_op jit(solution)/shard_map/all_gather | solution.py:29
  1044.3 11.9 reduce_sum.75
  1056.9 12.3 all_gather.75
  1071.3 112.8 %all-gather.26.cloned.1.call-done = f32[32768,256]{1,0:T(8,128)} async-done(((f32[1024,256]{1,0:T(8,128)}), f32[32768,256]{1,0:T(8,128)}) %all-gather.26.cloned.1.call-update) | async-done | bytes 33554448 | tf_op jit(solution)/shard_map/all_gather | solution.py:29
  1184.1 11.9 reduce_sum.76
  1196.6 12.3 all_gather.78
  1211.0 112.8 %all-gather.28.cloned.1.call-done = f32[32768,256]{1,0:T(8,128)} async-done(((f32[1024,256]{1,0:T(8,128)}), f32[32768,256]{1,0:T(8,128)}) %all-gather.28.cloned.1.call-update) | async-done | bytes 33554448 | tf_op jit(solution)/shard_map/all_gather | solution.py:29
  1323.9 11.9 reduce_sum.77
  1336.4 12.3 all_gather.81
  1351.5 112.1 %all-gather.30.cloned.1.call-done = f32[32768,256]{1,0:T(8,128)} async-done(((f32[1024,256]{1,0:T(8,128)}), f32[32768,256]{1,0:T(8,128)}) %all-gather.30.cloned.1.call-update) | async-done | bytes 33554448 | tf_op jit(solution)/shard_map/all_gather | solution.py:29
  1463.6 11.9 reduce_sum.78
  (85 shorter events, 50.7 us)
Async XLA Ops:
  7.2 48.0 %all-gather.18.cloned.1.call-start = ((), (), s32[]{:S(2)}) async-start(), calls=%async_computation.2 | async-start | bytes 1081344 | tf_op jit(solution)/shard_map/all_gather | solution.py:34
  7.9 167.1 %all-gather.16.cloned.1.call-start = ((), (), s32[]{:S(2)}) async-start(), calls=%async_computation.1 | async-start | bytes 15728640 | tf_op jit(solution)/shard_map/all_gather | solution.py:33
  8.6 363.7 %all-reduce.4.cloned.1.call-start = ((), (), s32[]{:S(2)}) async-start(), calls=%async_computation.10 | async-start | bytes 524288
  252.2 8.2 copy-start.1
  252.2 8.9 copy-start
  260.4 311.9 %reduce-scatter.4.cloned.1.call-start = ((), (), s32[]{:S(2)}) async-start(), calls=%async_computation.9 | async-start | bytes 1081344 | tf_op jit(solution)/shard_map/reduce_scatter | solution.py:88
  495.7 269.2 %all-gather.20.cloned.1.call-start = ((), (), s32[]{:S(2)}) async-start(), calls=%async_computation.3 | async-start | bytes 34603008 | tf_op jit(solution)/shard_map/all_gather | solution.py:29
  651.6 253.0 %all-gather.22.cloned.1.call-start = ((), (), s32[]{:S(2)}) async-start(), calls=%async_computation.4 | async-start | bytes 34603008 | tf_op jit(solution)/shard_map/all_gather | solution.py:29
  791.7 252.6 %all-gather.24.cloned.1.call-start = ((), (), s32[]{:S(2)}) async-start(), calls=%async_computation.5 | async-start | bytes 34603008 | tf_op jit(solution)/shard_map/all_gather | solution.py:29
  931.5 252.6 %all-gather.26.cloned.1.call-start = ((), (), s32[]{:S(2)}) async-start(), calls=%async_computation.6 | async-start | bytes 34603008 | tf_op jit(solution)/shard_map/all_gather | solution.py:29
  1071.2 252.6 %all-gather.28.cloned.1.call-start = ((), (), s32[]{:S(2)}) async-start(), calls=%async_computation.7 | async-start | bytes 34603008 | tf_op jit(solution)/shard_map/all_gather | solution.py:29
  1211.0 252.6 %all-gather.30.cloned.1.call-start = ((), (), s32[]{:S(2)}) async-start(), calls=%async_computation.8 | async-start | bytes 34603008 | tf_op jit(solution)/shard_map/all_gather | solution.py:29
Sparse Core Ops, SparseCore 0:
  10.3 44.8 all-gather.17
  56.8 118.0 all-gather.15
  260.5 103.2 all-reduce.3
  495.8 76.4 reduce-scatter.3
  651.7 113.0 all-gather.19
  791.9 112.6 all-gather.21
  931.6 112.6 all-gather.23
  1071.4 112.6 all-gather.25
  1211.1 112.6 all-gather.27
  1350.9 112.6 all-gather.29
